TPU v7x, 32 devices: a whole 2x2x4 slice. The times are simulated.
32 devices in a mesh: grp: 4 (over z), mem: 8 (over y, x, core).
Axes of the slice: x: 2, y: 2, z: 4, core: 2. Of those that a mesh axis runs over, the one named last changes fastest.
Arguments:
- child_means: float32 [65536, 64], P(('grp', 'mem')), may hold values from -48 to 48
- child_variances: float32 [65536, 64], P(('grp', 'mem')), may hold values from 0.2 to 2
- virtual_counts: int32 [65536], P(('grp', 'mem')), may hold values from 1 to 4
- assignment: int32 [65536, 1], P(('grp', 'mem')), may hold values from 0 to 511
Outputs:
- parent_means: float32 [512, 64], P('mem')
- parent_variances: float32 [512, 64], P('mem')
- parent_weights: float32 [512], P('mem')
All inputs are finite; a program needn't handle non-finite values.
Results may differ from a plain program's by a relative error of at most 0.0003.
Values sent between devices are 32-bit elements; how exact they have to be, the bound alone decides.
A program may use at most 64 MiB of HBM per device.

v0:
```python
import math
import jax
import jax.numpy as jnp
from jax import lax
from jax.sharding import PartitionSpec as P

P_SIZE = 512
ITERS = 2


def child_features(means, variances):
    return jnp.concatenate([means, variances + means * means], axis=1)


def accumulate(features, extras, weigh):
    row_count = features.shape[0]
    block = math.gcd(row_count, 1024)
    turns = row_count // block
    pieces = (features.reshape(turns, block, features.shape[1]),) + tuple(
        (extra.reshape((turns, block) + extra.shape[1:]) for extra in extras)
    )

    def advance(carry, piece):
        weights = weigh(*piece)
        sums = carry[0] + lax.dot_general(
            weights,
            piece[0],
            (((0,), (0,)), ((), ())),
            precision=lax.Precision.HIGHEST,
            preferred_element_type=jnp.float32,
        )
        counts = carry[1] + jnp.sum(weights, axis=0)
        return ((sums, counts), None)

    start_sums = (
        jnp.zeros((P_SIZE, features.shape[1]), jnp.float32),
        jnp.zeros((P_SIZE,), jnp.float32),
    )
    return lax.scan(advance, start_sums, pieces)[0]


def maximize(counts, sums, total):
    width = sums.shape[1] // 2
    mass = counts + 1.0
    means = sums[:, :width] / mass[:, None]
    second = (sums[:, width:] + 1.0) / mass[:, None]
    return (means, second - means * means, mass / (total + P_SIZE))


def parent_table(means, variances, weights):
    inverse = 1.0 / variances
    table = jnp.concatenate([-2.0 * means * inverse, inverse], axis=1)
    offset = jnp.sum(jnp.log(2.0 * math.pi * variances) + means * means * inverse, axis=1)
    return (table, offset, jnp.log(weights))


def soft_weights(block_features, block_virtual, table, offset, log_weight):
    width = block_features.shape[1] // 2
    cross = lax.dot_general(
        block_features,
        table,
        (((1,), (1,)), ((), ())),
        precision=lax.Precision.HIGHEST,
        preferred_element_type=jnp.float32,
    )
    ell = -0.5 / width * (cross + offset[None, :])
    score = log_weight[None, :] + block_virtual[:, None] * ell
    top = jnp.max(score, axis=1, keepdims=True)
    expd = jnp.exp(score - top)
    resp = expd / jnp.sum(expd, axis=1, keepdims=True)
    return resp * block_virtual[:, None]


def shards(child_means, child_variances, virtual_counts, assignment):
    features = child_features(child_means, child_variances)
    virtual = virtual_counts.astype(jnp.float32)
    labels = jnp.arange(P_SIZE, dtype=jnp.int32)

    def initial_weights(block_features, block_virtual, block_assign):
        return (block_assign == labels[None, :]).astype(jnp.float32) * block_virtual[:, None]

    sums, counts = accumulate(features, (virtual, assignment), initial_weights)
    total = lax.psum(jnp.sum(virtual), ("grp", "mem"))

    def combine(local_sums, local_counts):
        shared = (
            lax.psum_scatter(local_sums, "mem", scatter_dimension=0, tiled=True),
            lax.psum_scatter(local_counts, "mem", scatter_dimension=0, tiled=True),
        )
        return lax.psum((shared[0], shared[1]), "grp")

    own_sums, own_counts = combine(sums, counts)
    means, variances, weights = maximize(own_counts, own_sums, total)
    for iteration in range(ITERS):
        all_means, all_variances, all_weights = (
            lax.all_gather(means, "mem", axis=0, tiled=True),
            lax.all_gather(variances, "mem", axis=0, tiled=True),
            lax.all_gather(weights, "mem", axis=0, tiled=True),
        )
        table, offset, log_weight = parent_table(all_means, all_variances, all_weights)

        def weigh(block_features, block_virtual):
            return soft_weights(block_features, block_virtual, table, offset, log_weight)

        sums, counts = accumulate(features, (virtual,), weigh)
        own_sums, own_counts = combine(sums, counts)
        means, variances, weights = maximize(own_counts, own_sums, total)
    return (means, variances, weights)


def solution(mesh):
    in_specs = (
        P(("grp", "mem"), None),
        P(("grp", "mem"), None),
        P(("grp", "mem")),
        P(("grp", "mem"), None),
    )
    out_specs = (P("mem", None), P("mem", None), P("mem"))
    return jax.shard_map(shards, mesh=mesh, in_specs=in_specs, out_specs=out_specs, check_vma=False)
```

profile of v0, /device:TPU:0, one launch (start us, length us, event | category | flops | bytes accessed | tf_op | source)
XLA Modules:
  0.0 293.5 jit_solution(11252077472539837460)
XLA Ops:
  10.1 8.4 %while.39 = (s32[]{:T(128)}, f32[512,128]{1,0:T(8,128)S(1)}, f32[512]{0:T(512)S(1)}, s32[2,1024,1]{1,2,0:T(1,128)S(1)}, f32[2,1024]{1,0:T(2,128)S(1)}, /*index=5*/f32[2,1024,128]{2,1,0:T(8,128)S(1)}, s32[]{:T(128)}, s32[]{:T(128)}) while((s32[]{:T(128)}, f32[512,128]{1,0:T(8,128)S(1)}, f32[512]{0:T(512)S(1)}, ...), condition=%wide.region_2.3_spmd.clone, body=%wide.region_0.2_spmd.clone.sunk | while | flops 808059392 | bytes 1089644 | solution.py:39
  10.1 3.8 %fusion.56 = f32[512,128]{1,0:T(8,128)S(1)} fusion(f32[1024]{0:T(1024)S(1)} %bitcast.56, s32[1024]{0:T(1024)S(1)} %bitcast.58, f32[2,1024,128]{2,1,0:T(8,128)S(1)} %get-tuple-element.448, s32[]{:T(128)} %get-tuple-element.435, f32[512,128]{1,0:T(8,128)S(1)} %get-tuple-element.436, pred[]{:T(512)S(6)} %compare.9), kind=kOutput, calls=%fused_computation.5.clone.1 | convolution fusion | flops 806486016 | bytes 1056773 | tf_op jit(solution)/shard_map/while/body/eval_jaxpr/dot_general | solution.py:25
  14.3 3.8 %fusion.56 = f32[512,128]{1,0:T(8,128)S(1)} fusion(f32[1024]{0:T(1024)S(1)} %bitcast.56, s32[1024]{0:T(1024)S(1)} %bitcast.58, f32[2,1024,128]{2,1,0:T(8,128)S(1)} %get-tuple-element.448, s32[]{:T(128)} %get-tuple-element.435, f32[512,128]{1,0:T(8,128)S(1)} %get-tuple-element.436, pred[]{:T(512)S(6)} %compare.9), kind=kOutput, calls=%fused_computation.5.clone.1 | convolution fusion | flops 806486016 | bytes 1056773 | tf_op jit(solution)/shard_map/while/body/eval_jaxpr/dot_general | solution.py:25
  19.8 42.2 %psum.50 = f32[]{:T(128)} all-reduce(f32[]{:T(128)} %convert_reduce_fusion), channel_id=1, replica_groups=mesh['grp'=4,'mem'=8] {'grp','mem'}, use_global_device_ids=true, to_apply=%region_9.10 | all-reduce | flops 1 | bytes 8 | tf_op jit(solution)/shard_map/psum | solution.py:83
  63.2 13.0 %all-reduce.2 = f32[512]{0:T(512)S(1)} all-reduce(f32[512]{0:T(512)S(1)} %get-tuple-element.127), channel_id=2, replica_groups=mesh['grp'=4,'mem'=8] {'mem'}, use_global_device_ids=true, to_apply=%region_5.6.clone | all-reduce | flops 512 | bytes 4096
  77.6 18.8 %all-reduce.7 = (f32[64]{0:T(128)S(1)}, f32[64,128]{1,0:T(8,128)S(1)}) all-reduce(f32[64]{0:T(128)S(1)} %dynamic-slice.3, f32[64,128]{1,0:T(8,128)} %reduce-scatter.4.cloned.1.call-done), channel_id=1, replica_groups=mesh['grp'=4,'mem'=8] {'grp'}, use_global_device_ids=true, to_apply=%region_6.7 | all-reduce | flops 8256 | bytes 66048 | tf_op jit(solution)/shard_map/psum | solution.py:90
  96.6 9.1 %all_gather.19 = f32[512,64]{1,0:T(8,128)S(1)} all-gather(f32[64,64]{1,0:T(8,128)S(1)} %get-tuple-element.274), channel_id=1, replica_groups=mesh['grp'=4,'mem'=8] {'mem'}, dimensions={0}, use_global_device_ids=true | all-gather | bytes 147456 | tf_op jit(solution)/shard_map/all_gather | solution.py:96
  105.7 8.5 %all_gather.20 = f32[512,64]{1,0:T(8,128)S(1)} all-gather(f32[64,64]{1,0:T(8,128)S(1)} %get-tuple-element.275), channel_id=1, replica_groups=mesh['grp'=4,'mem'=8] {'mem'}, dimensions={0}, use_global_device_ids=true | all-gather | bytes 147456 | tf_op jit(solution)/shard_map/all_gather | solution.py:97
  114.2 13.4 %all-reduce = f32[512]{0:T(512)S(1)} all-reduce(f32[512]{0:T(512)S(1)} %get-tuple-element.281), channel_id=1, replica_groups=mesh['grp'=4,'mem'=8] {'mem'}, use_global_device_ids=true, to_apply=%add | all-reduce | flops 512 | bytes 4096
  127.9 12.2 %while.40 = (s32[]{:T(128)}, f32[512,128]{1,0:T(8,128)}, f32[512]{0:T(512)S(1)}, f32[512]{0:T(512)S(1)}, f32[2,1024,128]{2,1,0:T(8,128)S(1)}, /*index=5*/f32[512...) while((s32[]{:T(128)}, f32[512,128]{1,0:T(8,128)}, ...), condition=%wide.region_14.15_spmd.clone, body=%wide.region_10.14_spmd.clone.sunk | while | flops 1617559040 | bytes 10293372 | solution.py:39
  130.8 2.7 convolution_add_fusion.4
  136.5 3.7 %convolution_add_fusion.4 = f32[512,128]{1,0:T(8,128)} fusion(f32[2,1024,128]{2,1,0:T(8,128)S(1)} %get-tuple-element.475, s32[]{:T(128)} %get-tuple-element.461, f32[1024,512]{0,1:T(8,128)S(1)} %get-tuple-element.415, f32[1024]{0:T(1024)S(1)} %bitcast.52, f32[1024]{0:T(1024)S(1)} %fusion.60, f32[1024]{0:T(1024)S(1)} %get-tuple-element.416, ...), kind=kOutput, calls=%fused_computation.20.clone.1 | convolution fusion | flops 807010304 | bytes 3158021 | tf_op jit(solution)/shard_map/while/body/eval_jaxpr/dot_general | solution.py:25
  140.2 11.8 %all-reduce.3 = f32[512]{0:T(512)S(1)} all-reduce(f32[512]{0:T(512)S(1)} %get-tuple-element.129), channel_id=4, replica_groups=mesh['grp'=4,'mem'=8] {'mem'}, use_global_device_ids=true, to_apply=%region_17.18.clone | all-reduce | flops 512 | bytes 4096
  152.1 19.0 %reduce-scatter.6.cloned.1.call-done = f32[64,128]{1,0:T(8,128)} async-done(((f32[512,128]{1,0:T(8,128)}), f32[64,128]{1,0:T(8,128)}) %reduce-scatter.6.cloned.1.call-update) | async-done | bytes 32784 | tf_op jit(solution)/shard_map/reduce_scatter | solution.py:87
  171.1 19.9 %all-reduce.6 = (f32[64]{0:T(128)S(1)}, f32[64,128]{1,0:T(8,128)S(1)}) all-reduce(f32[64]{0:T(128)S(1)} %dynamic-slice.5, f32[64,128]{1,0:T(8,128)} %reduce-scatter.6.cloned.1.call-done), channel_id=1, replica_groups=mesh['grp'=4,'mem'=8] {'grp'}, use_global_device_ids=true, to_apply=%region_18.19 | all-reduce | flops 8256 | bytes 66048 | tf_op jit(solution)/shard_map/psum | solution.py:90
  191.2 9.3 %all_gather.22 = f32[512,64]{1,0:T(8,128)S(1)} all-gather(f32[64,64]{1,0:T(8,128)S(1)} %get-tuple-element.272), channel_id=1, replica_groups=mesh['grp'=4,'mem'=8] {'mem'}, dimensions={0}, use_global_device_ids=true | all-gather | bytes 147456 | tf_op jit(solution)/shard_map/all_gather | solution.py:96
  200.4 8.3 %all_gather.23 = f32[512,64]{1,0:T(8,128)S(1)} all-gather(f32[64,64]{1,0:T(8,128)S(1)} %get-tuple-element.273), channel_id=1, replica_groups=mesh['grp'=4,'mem'=8] {'mem'}, dimensions={0}, use_global_device_ids=true | all-gather | bytes 147456 | tf_op jit(solution)/shard_map/all_gather | solution.py:97
  208.8 13.4 %all-reduce.1 = f32[512]{0:T(512)S(1)} all-reduce(f32[512]{0:T(512)S(1)} %get-tuple-element.279), channel_id=1, replica_groups=mesh['grp'=4,'mem'=8] {'mem'}, use_global_device_ids=true, to_apply=%add.1 | all-reduce | flops 512 | bytes 4096
  222.5 12.2 %while.41 = (s32[]{:T(128)}, f32[512,128]{1,0:T(8,128)}, f32[512]{0:T(512)S(1)}, f32[512]{0:T(512)S(1)}, f32[2,1024,128]{2,1,0:T(8,128)S(1)}, /*index=5*/f32[512...) while((s32[]{:T(128)}, f32[512,128]{1,0:T(8,128)}, ...), condition=%wide.region_24.25_spmd.clone, body=%wide.region_20.24_spmd.clone.sunk | while | flops 1617559040 | bytes 10293372 | solution.py:39
  225.4 2.7 convolution_add_fusion.5
  231.1 3.7 %convolution_add_fusion.5 = f32[512,128]{1,0:T(8,128)} fusion(f32[2,1024,128]{2,1,0:T(8,128)S(1)} %get-tuple-element.505, s32[]{:T(128)} %get-tuple-element.491, f32[1024,512]{0,1:T(8,128)S(1)} %get-tuple-element.425, f32[1024]{0:T(1024)S(1)} %bitcast.55, f32[1024]{0:T(1024)S(1)} %fusion.65, f32[1024]{0:T(1024)S(1)} %get-tuple-element.426, ...), kind=kOutput, calls=%fused_computation.35.clone.1 | convolution fusion | flops 807010304 | bytes 3158021 | tf_op jit(solution)/shard_map/while/body/eval_jaxpr/dot_general | solution.py:25
  234.7 11.8 %all-reduce.4 = f32[512]{0:T(512)S(1)} all-reduce(f32[512]{0:T(512)S(1)} %get-tuple-element.132), channel_id=7, replica_groups=mesh['grp'=4,'mem'=8] {'mem'}, use_global_device_ids=true, to_apply=%region_27.28.clone | all-reduce | flops 512 | bytes 4096
  246.6 19.2 %reduce-scatter.8.cloned.1.call-done = f32[64,128]{1,0:T(8,128)} async-done(((f32[512,128]{1,0:T(8,128)}), f32[64,128]{1,0:T(8,128)}) %reduce-scatter.8.cloned.1.call-update) | async-done | bytes 32784 | tf_op jit(solution)/shard_map/reduce_scatter | solution.py:87
  265.8 19.9 %all-reduce.5 = (f32[64,128]{1,0:T(8,128)S(1)}, f32[64]{0:T(128)S(1)}) all-reduce(f32[64,128]{1,0:T(8,128)} %reduce-scatter.8.cloned.1.call-done, f32[64]{0:T(128)S(1)} %dynamic-slice.7), channel_id=1, replica_groups=mesh['grp'=4,'mem'=8] {'grp'}, use_global_device_ids=true, to_apply=%region_26.27 | all-reduce | flops 8256 | bytes 66048 | tf_op jit(solution)/shard_map/psum | solution.py:90
  (77 shorter events, 19.7 us)
Async XLA Ops:
  7.2 70.4 %reduce-scatter.4.cloned.1.call-start = ((), (), s32[]{:S(2)}) async-start(), calls=%async_computation.3 | async-start | bytes 294912 | tf_op jit(solution)/shard_map/reduce_scatter | solution.py:87
  8.5 1.5 copy-start.2
  8.5 1.5 copy-start.1
  10.1 51.9 %copy-start.3 = (u32[32]{0:T(128)S(1)}, u32[32]{0:T(128)}, u32[]{:S(2)}) copy-start(u32[32]{0:T(128)} %constant.58) | copy-start | bytes 388
  18.5 0.7 copy-start
  19.2 151.9 %reduce-scatter.6.cloned.1.call-start = ((), (), s32[]{:S(2)}) async-start(), calls=%async_computation.4 | async-start | bytes 294912 | tf_op jit(solution)/shard_map/reduce_scatter | solution.py:87
  140.1 125.7 %reduce-scatter.8.cloned.1.call-start = ((), (), s32[]{:S(2)}) async-start(), calls=%async_computation.5 | async-start | bytes 294912 | tf_op jit(solution)/shard_map/reduce_scatter | solution.py:87
Sparse Core Ops, SparseCore 0:
  19.3 36.3 reduce-scatter.3
  140.3 30.7 reduce-scatter.5
  234.9 30.9 reduce-scatter.7
where the time goes:
time: 294 us; the launch traced here: 293 us
  blocking collectives  199 us (68%)
  waiting for transfers between devices  38.3 us (13%)
  matrix products  28.4 us (10%)
  between operations  15.9 us (5%)
  other arithmetic  9.37 us (3%)
    unnamed x5, blocking collectives  63.3 us
    psum x3, blocking collectives, combine(): return lax.psum((shared[0], shared[1]), 'grp')  58.5 us
    psum x1, blocking collectives, shards(): total = lax.psum(jnp.sum(virtual), ('grp', 'mem'))  42.2 us
    reduce_scatter x3, waiting for transfers between devices, combine(): lax.psum_scatter(local_sums, 'mem', scatter_dimension=0, tiled=True)  38.2 us
    dot_general x6, matrix products, advance(): lax.dot_general(weights, piece[0], (((0,), (0,)), ((), ())), precision=la...  20.3 us
    all_gather x2, blocking collectives, shards(): lax.all_gather(means, 'mem', axis=0, tiled=True)  18.4 us
    all_gather x2, blocking collectives, shards(): lax.all_gather(variances, 'mem', axis=0, tiled=True)  16.8 us
    dot_general x4, matrix products, soft_weights(): lax.dot_general(block_features, table, (((1,), (1,)), ((), ())), precisio...  8.14 us
  transfers between devices with their start and end apart: 3, of which 2 were waited for; matrix products, arithmetic and copies ran while one was open for 0% of the time, Pallas kernels for 0%

commit v1 on v0

--- a/solution.py
+++ b/solution.py
@@ -6,6 +6,28 @@
 
 P_SIZE = 512
 ITERS = 2
+
+
+def in_order(blocks, dim):
+    blocks = jnp.moveaxis(blocks, 0, dim)
+    shape = blocks.shape
+    return blocks.reshape(*shape[:dim], shape[dim] * shape[dim + 1], *shape[dim + 2 :])
+
+
+def collected_by_bits(value, axis):
+    size = lax.axis_size(axis)
+    parts = value[None]
+    for level in range(size.bit_length() - 1):
+        bit = 1 << level
+        theirs = lax.ppermute(parts, axis, [(i, i ^ bit) for i in range(size)])
+        both = jnp.stack([parts, theirs])
+        upper = lax.axis_index(axis) >> level & 1
+        parts = jnp.where(upper == 0, both, both[::-1]).reshape(-1, *value.shape)
+    return parts
+
+
+def collect(x, axis, dim):
+    return in_order(collected_by_bits(x, axis), dim)
 
 
 def child_features(means, variances):
@@ -94,7 +116,7 @@
     for iteration in range(ITERS):
         all_means, all_variances, all_weights = (
             lax.all_gather(means, "mem", axis=0, tiled=True),
-            lax.all_gather(variances, "mem", axis=0, tiled=True),
+            collect(variances, "mem", 0),
             lax.all_gather(weights, "mem", axis=0, tiled=True),
         )
         table, offset, log_weight = parent_table(all_means, all_variances, all_weights)

time: 294 us -> 288 us (0.980)
  blocking collectives: 199 us -> 181 us
  waiting for transfers between devices: 38.3 us -> 45.1 us
  starting transfers between devices: 0.12 us -> 4.85 us
    all_gather x2 -> x0, blocking collectives: 16.8 us -> none  [shards(): lax.all_gather(variances, 'mem', axis=0, tiled=True)]
    ppermute x0 -> x6, waiting for transfers between devices: none -> 9.43 us  [collected_by_bits(): theirs = lax.ppermute(parts, axis, [(i, i ^ bit) for i in range(size)])]
    ppermute x0 -> x6, starting transfers between devices: none -> 4.73 us  [collected_by_bits(): theirs = lax.ppermute(parts, axis, [(i, i ^ bit) for i in range(size)])]
  transfers between devices with their start and end apart: 3 -> 9, of which waited for: 2 -> 6; matrix products, arithmetic and copies ran while one was open for 0% -> 1% of each run, Pallas kernels for 0% -> 0%
where the time goes in v1:
time: 288 us; the launch traced here: 287 us
  blocking collectives  181 us (63%)
  waiting for transfers between devices  45.1 us (16%)
  matrix products  28.4 us (10%)
  between operations  16 us (6%)
  other arithmetic  9.61 us (3%)
  starting transfers between devices  4.85 us (2%)
    unnamed x5, blocking collectives  62.9 us
    psum x3, blocking collectives, combine(): return lax.psum((shared[0], shared[1]), 'grp')  58.4 us
    psum x1, blocking collectives, shards(): total = lax.psum(jnp.sum(virtual), ('grp', 'mem'))  42.2 us
    reduce_scatter x3, waiting for transfers between devices, combine(): lax.psum_scatter(local_sums, 'mem', scatter_dimension=0, tiled=True)  35.6 us
    dot_general x6, matrix products, advance(): lax.dot_general(weights, piece[0], (((0,), (0,)), ((), ())), precision=la...  20.3 us
    all_gather x2, blocking collectives, shards(): lax.all_gather(means, 'mem', axis=0, tiled=True)  17.2 us
    ppermute x6, waiting for transfers between devices, collected_by_bits(): theirs = lax.ppermute(parts, axis, [(i, i ^ bit) for i in range(size)])  9.43 us
    dot_general x4, matrix products, soft_weights(): lax.dot_general(block_features, table, (((1,), (1,)), ((), ())), precisio...  8.15 us
  transfers between devices with their start and end apart: 9, of which 6 were waited for; matrix products, arithmetic and copies ran while one was open for 1% of the time, Pallas kernels for 0%

profile of v1, /device:TPU:0, one launch (start us, length us, event | category | flops | bytes accessed | tf_op | source)
XLA Modules:
  0.0 286.9 jit_solution(17092758935250527949)
XLA Ops:
  10.1 8.4 %while.39 = (s32[]{:T(128)}, f32[512,128]{1,0:T(8,128)S(1)}, f32[512]{0:T(512)S(1)}, s32[2,1024,1]{1,2,0:T(1,128)S(1)}, f32[2,1024]{1,0:T(2,128)S(1)}, /*index=5*/f32[2,1024,128]{2,1,0:T(8,128)S(1)}, s32[]{:T(128)}, s32[]{:T(128)}) while((s32[]{:T(128)}, f32[512,128]{1,0:T(8,128)S(1)}, f32[512]{0:T(512)S(1)}, ...), condition=%wide.region_2.3_spmd.clone, body=%wide.region_0.2_spmd.clone.sunk | while | flops 808059392 | bytes 1089644 | solution.py:61
  10.1 3.8 %fusion.68 = f32[512,128]{1,0:T(8,128)S(1)} fusion(f32[1024]{0:T(1024)S(1)} %bitcast.110, s32[1024]{0:T(1024)S(1)} %bitcast.112, f32[2,1024,128]{2,1,0:T(8,128)S(1)} %get-tuple-element.456, s32[]{:T(128)} %get-tuple-element.443, f32[512,128]{1,0:T(8,128)S(1)} %get-tuple-element.444, pred[]{:T(512)S(6)} %compare.9), kind=kOutput, calls=%fused_computation.5.clone.1 | convolution fusion | flops 806486016 | bytes 1056773 | tf_op jit(solution)/shard_map/while/body/eval_jaxpr/dot_general | solution.py:47
  14.3 3.8 %fusion.68 = f32[512,128]{1,0:T(8,128)S(1)} fusion(f32[1024]{0:T(1024)S(1)} %bitcast.110, s32[1024]{0:T(1024)S(1)} %bitcast.112, f32[2,1024,128]{2,1,0:T(8,128)S(1)} %get-tuple-element.456, s32[]{:T(128)} %get-tuple-element.443, f32[512,128]{1,0:T(8,128)S(1)} %get-tuple-element.444, pred[]{:T(512)S(6)} %compare.9), kind=kOutput, calls=%fused_computation.5.clone.1 | convolution fusion | flops 806486016 | bytes 1056773 | tf_op jit(solution)/shard_map/while/body/eval_jaxpr/dot_general | solution.py:47
  19.8 42.2 %psum.50 = f32[]{:T(128)} all-reduce(f32[]{:T(128)} %convert_reduce_fusion), channel_id=1, replica_groups=mesh['grp'=4,'mem'=8] {'grp','mem'}, use_global_device_ids=true, to_apply=%region_9.10 | all-reduce | flops 1 | bytes 8 | tf_op jit(solution)/shard_map/psum | solution.py:105
  63.2 12.9 %all-reduce.2 = f32[512]{0:T(512)S(1)} all-reduce(f32[512]{0:T(512)S(1)} %get-tuple-element.127), channel_id=2, replica_groups=mesh['grp'=4,'mem'=8] {'mem'}, use_global_device_ids=true, to_apply=%region_5.6.clone | all-reduce | flops 512 | bytes 4096
  77.5 18.7 %all-reduce.7 = (f32[64]{0:T(128)S(1)}, f32[64,128]{1,0:T(8,128)S(1)}) all-reduce(f32[64]{0:T(128)S(1)} %dynamic-slice.3, f32[64,128]{1,0:T(8,128)} %reduce-scatter.4.cloned.1.call-done), channel_id=1, replica_groups=mesh['grp'=4,'mem'=8] {'grp'}, use_global_device_ids=true, to_apply=%region_6.7 | all-reduce | flops 8256 | bytes 66048 | tf_op jit(solution)/shard_map/psum | solution.py:112
  97.9 4.2 %collective-permute-done.1 = f32[2,64,64]{2,1,0:T(8,128)S(1)} collective-permute-done((f32[2,64,64]{2,1,0:T(8,128)S(1)}, f32[2,64,64]{2,1,0:T(8,128)S(1)}, u32[]{:S(2)}, u32[]{:S(2)}) %collective-permute-start.1) | collective-permute-done | bytes 32800 | tf_op jit(solution)/shard_map/ppermute | solution.py:22
  103.6 11.8 %all-reduce = f32[512]{0:T(512)S(1)} all-reduce(f32[512]{0:T(512)S(1)} %get-tuple-element.289), channel_id=1, replica_groups=mesh['grp'=4,'mem'=8] {'mem'}, use_global_device_ids=true, to_apply=%add | all-reduce | flops 512 | bytes 4096
  115.4 8.6 %all_gather.13 = f32[512,64]{1,0:T(8,128)S(1)} all-gather(f32[64,64]{1,0:T(8,128)S(1)} %get-tuple-element.281), channel_id=1, replica_groups=mesh['grp'=4,'mem'=8] {'mem'}, dimensions={0}, use_global_device_ids=true | all-gather | bytes 147456 | tf_op jit(solution)/shard_map/all_gather | solution.py:118
  124.4 12.2 %while.40 = (s32[]{:T(128)}, f32[512,128]{1,0:T(8,128)}, f32[512]{0:T(512)S(1)}, f32[512]{0:T(512)S(1)}, f32[2,1024,128]{2,1,0:T(8,128)S(1)}, /*index=5*/f32[512...) while((s32[]{:T(128)}, f32[512,128]{1,0:T(8,128)}, ...), condition=%wide.region_14.15_spmd.clone, body=%wide.region_10.14_spmd.clone.sunk | while | flops 1617559040 | bytes 10293372 | solution.py:61
  127.3 2.7 convolution_add_fusion.4
  133.0 3.7 %convolution_add_fusion.4 = f32[512,128]{1,0:T(8,128)} fusion(f32[2,1024,128]{2,1,0:T(8,128)S(1)} %get-tuple-element.483, s32[]{:T(128)} %get-tuple-element.469, f32[1024,512]{0,1:T(8,128)S(1)} %get-tuple-element.423, f32[1024]{0:T(1024)S(1)} %bitcast.102, f32[1024]{0:T(1024)S(1)} %fusion.72, f32[1024]{0:T(1024)S(1)} %get-tuple-element.424, ...), kind=kOutput, calls=%fused_computation.20.clone.1 | convolution fusion | flops 807010304 | bytes 3158021 | tf_op jit(solution)/shard_map/while/body/eval_jaxpr/dot_general | solution.py:47
  136.7 13.2 %all-reduce.3 = f32[512]{0:T(512)S(1)} all-reduce(f32[512]{0:T(512)S(1)} %get-tuple-element.129), channel_id=4, replica_groups=mesh['grp'=4,'mem'=8] {'mem'}, use_global_device_ids=true, to_apply=%region_17.18.clone | all-reduce | flops 512 | bytes 4096
  150.0 17.8 %reduce-scatter.6.cloned.1.call-done = f32[64,128]{1,0:T(8,128)} async-done(((f32[512,128]{1,0:T(8,128)}), f32[64,128]{1,0:T(8,128)}) %reduce-scatter.6.cloned.1.call-update) | async-done | bytes 32784 | tf_op jit(solution)/shard_map/reduce_scatter | solution.py:109
  167.8 19.9 %all-reduce.6 = (f32[64]{0:T(128)S(1)}, f32[64,128]{1,0:T(8,128)S(1)}) all-reduce(f32[64]{0:T(128)S(1)} %dynamic-slice.5, f32[64,128]{1,0:T(8,128)} %reduce-scatter.6.cloned.1.call-done), channel_id=1, replica_groups=mesh['grp'=4,'mem'=8] {'grp'}, use_global_device_ids=true, to_apply=%region_18.19 | all-reduce | flops 8256 | bytes 66048 | tf_op jit(solution)/shard_map/psum | solution.py:112
  190.7 2.8 collective-permute-done.4
  195.0 11.8 %all-reduce.1 = f32[512]{0:T(512)S(1)} all-reduce(f32[512]{0:T(512)S(1)} %get-tuple-element.287), channel_id=1, replica_groups=mesh['grp'=4,'mem'=8] {'mem'}, use_global_device_ids=true, to_apply=%add.1 | all-reduce | flops 512 | bytes 4096
  206.8 8.6 %all_gather.15 = f32[512,64]{1,0:T(8,128)S(1)} all-gather(f32[64,64]{1,0:T(8,128)S(1)} %get-tuple-element.278), channel_id=1, replica_groups=mesh['grp'=4,'mem'=8] {'mem'}, dimensions={0}, use_global_device_ids=true | all-gather | bytes 147456 | tf_op jit(solution)/shard_map/all_gather | solution.py:118
  215.9 12.2 %while.41 = (s32[]{:T(128)}, f32[512,128]{1,0:T(8,128)}, f32[512]{0:T(512)S(1)}, f32[512]{0:T(512)S(1)}, f32[2,1024,128]{2,1,0:T(8,128)S(1)}, /*index=5*/f32[512...) while((s32[]{:T(128)}, f32[512,128]{1,0:T(8,128)}, ...), condition=%wide.region_24.25_spmd.clone, body=%wide.region_20.24_spmd.clone.sunk | while | flops 1617559040 | bytes 10293372 | solution.py:61
  218.8 2.7 convolution_add_fusion.5
  224.5 3.7 %convolution_add_fusion.5 = f32[512,128]{1,0:T(8,128)} fusion(f32[2,1024,128]{2,1,0:T(8,128)S(1)} %get-tuple-element.513, s32[]{:T(128)} %get-tuple-element.499, f32[1024,512]{0,1:T(8,128)S(1)} %get-tuple-element.433, f32[1024]{0:T(1024)S(1)} %bitcast.105, f32[1024]{0:T(1024)S(1)} %fusion.77, f32[1024]{0:T(1024)S(1)} %get-tuple-element.434, ...), kind=kOutput, calls=%fused_computation.35.clone.1 | convolution fusion | flops 807010304 | bytes 3158021 | tf_op jit(solution)/shard_map/while/body/eval_jaxpr/dot_general | solution.py:47
  228.1 13.2 %all-reduce.4 = f32[512]{0:T(512)S(1)} all-reduce(f32[512]{0:T(512)S(1)} %get-tuple-element.132), channel_id=7, replica_groups=mesh['grp'=4,'mem'=8] {'mem'}, use_global_device_ids=true, to_apply=%region_27.28.clone | all-reduce | flops 512 | bytes 4096
  241.4 17.8 %reduce-scatter.8.cloned.1.call-done = f32[64,128]{1,0:T(8,128)} async-done(((f32[512,128]{1,0:T(8,128)}), f32[64,128]{1,0:T(8,128)}) %reduce-scatter.8.cloned.1.call-update) | async-done | bytes 32784 | tf_op jit(solution)/shard_map/reduce_scatter | solution.py:109
  259.2 19.8 %all-reduce.5 = (f32[64,128]{1,0:T(8,128)S(1)}, f32[64]{0:T(128)S(1)}) all-reduce(f32[64,128]{1,0:T(8,128)} %reduce-scatter.8.cloned.1.call-done, f32[64]{0:T(128)S(1)} %dynamic-slice.7), channel_id=1, replica_groups=mesh['grp'=4,'mem'=8] {'grp'}, use_global_device_ids=true, to_apply=%region_26.27 | all-reduce | flops 8256 | bytes 66048 | tf_op jit(solution)/shard_map/psum | solution.py:112
  (99 shorter events, 27.0 us)
Async XLA Ops:
  7.2 70.4 %reduce-scatter.4.cloned.1.call-start = ((), (), s32[]{:S(2)}) async-start(), calls=%async_computation.3 | async-start | bytes 294912 | tf_op jit(solution)/shard_map/reduce_scatter | solution.py:109
  8.5 1.5 copy-start.2
  8.5 1.6 copy-start.1
  10.1 51.9 %copy-start.3 = (u32[32]{0:T(128)S(1)}, u32[32]{0:T(128)}, u32[]{:S(2)}) copy-start(u32[32]{0:T(128)} %constant.66) | copy-start | bytes 388
  18.5 0.7 copy-start
  19.2 148.6 %reduce-scatter.6.cloned.1.call-start = ((), (), s32[]{:S(2)}) async-start(), calls=%async_computation.4 | async-start | bytes 294912 | tf_op jit(solution)/shard_map/reduce_scatter | solution.py:109
  96.5 1.3 collective-permute-start
  97.8 4.3 %collective-permute-start.1 = (f32[2,64,64]{2,1,0:T(8,128)S(1)}, f32[2,64,64]{2,1,0:T(8,128)S(1)}, u32[]{:S(2)}, u32[]{:S(2)}) collective-permute-start(f32[2,64,64]{2,1,0:T(8,128)S(1)} %get-tuple-element.277), channel_id=1, source_target_pairs={{0,2},{1,3},{2,0},{3,1},{4,6},{5,7},{6,4},{7,5},{8,10},{9,11},{10,... | collective-permute-start | bytes 98312 | tf_op jit(solution)/shard_map/ppermute | solution.py:22
  102.1 21.8 %collective-permute-start.2 = (f32[4,64,64]{2,1,0:T(8,128)S(1)}, f32[4,64,64]{2,1,0:T(8,128)S(1)}, u32[]{:S(2)}, u32[]{:S(2)}) collective-permute-start(f32[4,64,64]{2,1,0:T(8,128)S(1)} %bitcast.106), channel_id=1, source_target_pairs={{0,4},{1,5},{2,6},{3,7},{4,0},{5,1},{6,2},{7,3},{8,12},{9,13},{10,... | collective-permute-start | bytes 196616 | tf_op jit(solution)/shard_map/ppermute | solution.py:22
  136.7 122.6 %reduce-scatter.8.cloned.1.call-start = ((), (), s32[]{:S(2)}) async-start(), calls=%async_computation.5 | async-start | bytes 294912 | tf_op jit(solution)/shard_map/reduce_scatter | solution.py:109
  187.8 1.3 collective-permute-start.3
  189.1 4.3 %collective-permute-start.4 = (f32[2,64,64]{2,1,0:T(8,128)S(1)}, f32[2,64,64]{2,1,0:T(8,128)S(1)}, u32[]{:S(2)}, u32[]{:S(2)}) collective-permute-start(f32[2,64,64]{2,1,0:T(8,128)S(1)} %get-tuple-element.275), channel_id=1, source_target_pairs={{0,2},{1,3},{2,0},{3,1},{4,6},{5,7},{6,4},{7,5},{8,10},{9,11},{10,... | collective-permute-start | bytes 98312 | tf_op jit(solution)/shard_map/ppermute | solution.py:22
  193.5 22.0 %collective-permute-start.5 = (f32[4,64,64]{2,1,0:T(8,128)S(1)}, f32[4,64,64]{2,1,0:T(8,128)S(1)}, u32[]{:S(2)}, u32[]{:S(2)}) collective-permute-start(f32[4,64,64]{2,1,0:T(8,128)S(1)} %bitcast.108), channel_id=1, source_target_pairs={{0,4},{1,5},{2,6},{3,7},{4,0},{5,1},{6,2},{7,3},{8,12},{9,13},{10,... | collective-permute-start | bytes 196616 | tf_op jit(solution)/shard_map/ppermute | solution.py:22
Sparse Core Ops, SparseCore 0:
  19.3 36.3 reduce-scatter.3
  136.8 30.9 reduce-scatter.5
  228.3 30.9 reduce-scatter.7
